TPU v7x, 128 devices: a whole 4x4x4 slice. The times are simulated.
128 devices in a mesh: gz: 4 (over y_lo, core), gy: 32 (over z, y_hi, x).
Axes of the slice: x: 4, y: 4 (y_hi: 2, y_lo: 2; y = y_hi * 2 + y_lo), z: 4, core: 2. Of those that a mesh axis runs over, the one named last changes fastest.
Arguments:
- input_field: float32 [32, 16, 256, 256], P(None, 'gz', 'gy'), may hold values from -6 to 6
- pre_activation: float32 [32, 16, 256, 256], P(None, 'gz', 'gy'), may hold values from -8 to 8
- cotangent: float32 [32, 16, 256, 256], P(None, 'gz', 'gy'), may hold values from -6 to 6
- spectral_weights: float32 [2, 16, 32, 32, 32, 32], P(None, None, 'gz', 'gy'), may hold values from -4.2426405 to 4.2426405
- mix_weights: float32 [32, 32], replicated, may hold values from -1 to 1
- coefficients: float32 [5, 32], replicated, may hold values from -3 to 3
Outputs:
- grad_input: float32 [32, 16, 256, 256], P(None, 'gz', 'gy')
- grad_spectral: float32 [2, 16, 32, 32, 32, 32], P(None, None, 'gz', 'gy')
- grad_mix: float32 [32, 32], replicated
- grad_coef: float32 [5, 32], replicated
All inputs are finite; a program needn't handle non-finite values.
Results may differ from a plain program's by a relative error of at most 0.00013.
Values sent between devices are 32-bit elements; how exact they have to be, the bound alone decides.
A program may use at most 192 MiB of HBM per device.

v0:
```python
import functools
import math

import jax
import jax.numpy as jnp
import numpy as np
from jax import lax
from jax.experimental import pallas as pl
from jax.experimental.pallas import tpu as pltpu
from jax.sharding import PartitionSpec as P

F32 = jnp.float32
BF16 = jnp.bfloat16
MESH = pl.DeviceIdType.MESH
C = 32
ZL = 4
YL = 8
NX = 256
LANES = 128
NK = 128


def mode_numbers(number):
    positions = np.arange(number)
    return np.where(positions < number // 2, positions, positions - number)


def table(cells, modes):
    product = np.remainder(np.outer(mode_numbers(modes), np.arange(cells)), cells)
    angles = product * (2.0 * math.pi / cells)
    return np.cos(angles), np.sin(angles)


def split(a):
    high = a.astype(BF16)
    return high, (a - high.astype(F32)).astype(BF16)


def dot1(a, b, dims):
    return lax.dot_general(a, b, (dims, ((), ())), preferred_element_type=F32)


def dot3(a, b, dims):
    a_high, a_low = a if isinstance(a, tuple) else split(a)
    b_high, b_low = b if isinstance(b, tuple) else split(b)
    return dot1(a_high, b_low, dims) + dot1(a_low, b_high, dims) + dot1(a_high, b_high, dims)


NN = ((1,), (0,))
NT = ((1,), (1,))
TN = ((0,), (0,))


def gelu_slope(values):
    normal_cdf = 0.5 * (1.0 + lax.erf(values * 0.7071067811865476))
    return normal_cdf + values * jnp.exp(-0.5 * values * values) * 0.3989422804014327


def dft4(re, im, sign):
    ar, ai = re[0] + re[2], im[0] + im[2]
    br, bi = re[0] - re[2], im[0] - im[2]
    cr, ci = re[1] + re[3], im[1] + im[3]
    dr, di = re[1] - re[3], im[1] - im[3]
    if sign < 0:
        return [ar + cr, br + di, ar - cr, br - di], [ai + ci, bi - dr, ai - ci, bi + dr]
    return [ar + cr, br - di, ar - cr, br + di], [ai + ci, bi + dr, ai - ci, bi - dr]


def turn(re, im, cos, sin, sign):
    if sign < 0:
        return re * cos + im * sin, im * cos - re * sin
    return re * cos - im * sin, im * cos + re * sin


def plane(ref, start, size):
    return jnp.concatenate([ref[half, pl.ds(start, size), :] for half in range(2)], axis=1)


def put_plane(ref, start, value):
    for half in range(2):
        ref[half, pl.ds(start, value.shape[0]), :] = value[:, half * LANES : (half + 1) * LANES]


def iota(shape, axis):
    return lax.broadcasted_iota(jnp.int32, shape, axis)


def exchange_kernel(
    groups_y, groups_z, phases, cell_total,
    inp_hbm, pre_hbm, cot_hbm, wts_hbm, mix_ref, coef_ref, wx_ref, wy_ref, wyt_ref, tw_ref,
    lines_out, sten_out, hin_out, hsl_out, red_out,
    inp4, pre4, cot4, wts, inp2, slo2, sbuf, rbuf, zsend, zrecv, zsend2, zrecv2, sbuf2,
    hy_send, hy_recv, hz_recv, hid, sten, hin, hsl, hslt, dual, red_send, red_recv, red_sum,
    load_sem, s1, r1, s2, r2, sz, rz, sz2, rz2, hs_sem, hr_sem, sr, rr, out_sem,
):
    gz = lax.axis_index("gz")
    gy = lax.axis_index("gy")
    modes_x = wx_ref.shape[0] // 2

    def load(i, src, dst):
        return pltpu.make_async_copy(src, dst, load_sem.at[i])

    load(0, inp_hbm, inp4).start()
    load(1, pre_hbm, pre4).start()
    load(2, cot_hbm, cot4).start()

    barrier = pltpu.get_barrier_semaphore()

    def greet(i, carry):
        peer = lax.rem(gy + i, groups_y)
        pl.semaphore_signal(barrier, inc=1, device_id=(gz, peer), device_id_type=MESH)
        return carry

    lax.fori_loop(1, groups_y, greet, 0)
    for i in range(1, groups_z):
        peer = lax.rem(gz + i, groups_z)
        pl.semaphore_signal(barrier, inc=1, device_id=(peer, gy), device_id_type=MESH)

    wx = split(wx_ref[...])

    def along_x(source, field):
        cells = jnp.concatenate(
            [
                jnp.concatenate(
                    [source[half, pl.ds(y, LANES, stride=YL), :] for half in range(2)], axis=1
                )
                for y in range(YL)
            ],
            axis=0,
        )
        result = dot3(wx, cells, NT)
        for y in range(YL):
            for part in range(2):
                sbuf[pl.ds((2 * field + part) * YL + y, modes_x, stride=4 * YL), :] = (
                    result[part * modes_x : (part + 1) * modes_x, y * LANES : (y + 1) * LANES]
                )

    load(0, inp_hbm, inp4).wait()
    for z in range(ZL):
        put_plane(inp2, z * 256, inp4[:, z].reshape(256, NX))
    along_x(inp2, 0)
    load(1, pre_hbm, pre4).wait()
    load(2, cot_hbm, cot4).wait()
    load(3, wts_hbm, wts).start()

    def slope_step(step, carry):
        z = step // 4
        c = lax.rem(step, 4) * 8
        pre = pre4[pl.ds(c, 8), z].reshape(64, NX)
        cot = cot4[pl.ds(c, 8), z].reshape(64, NX)
        put_plane(slo2, pl.multiple_of(step * 64, 64), cot * gelu_slope(pre))
        return carry

    lax.fori_loop(0, 16, slope_step, 0)
    along_x(slo2, 1)
    for z in range(ZL):
        for side, y in enumerate((YL - 1, 0)):
            for half in range(2):
                hy_send[side, half, pl.ds(z * C, C), :] = slo2[
                    half, pl.ds(z * 256 + y, C, stride=YL), :
                ]

    pl.semaphore_wait(barrier, groups_y - 1 + groups_z - 1)

    def rows(ref, index, size=YL):
        return ref.at[pl.ds(pl.multiple_of(index * size, size), size), :]

    def first(i):
        peer = lax.rem(gy + i, groups_y)
        return pltpu.make_async_remote_copy(
            rows(sbuf, peer, 4 * YL), rows(rbuf, gy, 4 * YL), s1.at[peer], r1.at[gy],
            device_id=(gz, peer), device_id_type=MESH,
        )

    def first_in(i):
        peer = lax.rem(gy + i, groups_y)
        return pltpu.make_async_remote_copy(
            rows(sbuf, peer, 4 * YL), rows(rbuf, peer, 4 * YL), s1.at[peer], r1.at[peer],
            device_id=(gz, peer), device_id_type=MESH,
        )

    def second(i):
        peer = lax.rem(gy + i, groups_y)
        return pltpu.make_async_remote_copy(
            rows(sbuf2, peer, 2 * YL), rows(lines_out, gy, 2 * YL), s2.at[peer], r2.at[gy],
            device_id=(gz, peer), device_id_type=MESH,
        )

    def second_in(i):
        peer = lax.rem(gy + i, groups_y)
        return pltpu.make_async_remote_copy(
            rows(sbuf2, peer, 2 * YL), rows(lines_out, peer, 2 * YL), s2.at[peer], r2.at[peer],
            device_id=(gz, peer), device_id_type=MESH,
        )

    def across(source, target, send, recv, i, inward):
        peer = lax.rem(gz + i, groups_z)
        slot = peer if inward else gz
        return pltpu.make_async_remote_copy(
            rows(source, peer), rows(target, slot), send.at[peer], recv.at[slot],
            device_id=(peer, gy), device_id_type=MESH,
        )

    def each(make, action):
        def body(i, carry):
            getattr(make(i), action)()
            return carry

        lax.fori_loop(1, groups_y, body, 0)

    each(first, "start")
    own_lines = pl.ds(pl.multiple_of(gy * 4 * YL, 4 * YL), 4 * YL)
    rbuf[own_lines, :] = sbuf[own_lines, :]

    next_z, prev_z = lax.rem(gz + 1, groups_z), lax.rem(gz + groups_z - 1, groups_z)
    next_y, prev_y = lax.rem(gy + 1, groups_y), lax.rem(gy + groups_y - 1, groups_y)
    halos = []
    for i, (source, target, device) in enumerate(
        (
            (slo2.at[:, pl.ds(3 * 256, 256), :], hz_recv.at[0], (next_z, gy)),
            (slo2.at[:, pl.ds(0, 256), :], hz_recv.at[1], (prev_z, gy)),
            (hy_send.at[0], hy_recv.at[0], (gz, next_y)),
            (hy_send.at[1], hy_recv.at[1], (gz, prev_y)),
        )
    ):
        halos.append(
            pltpu.make_async_remote_copy(
                source, target, hs_sem.at[i], hr_sem.at[i], device_id=device, device_id_type=MESH
            )
        )
        halos[-1].start()

    has_before_z = jnp.where(gz > 0, 1.0, 0.0)
    has_after_z = jnp.where(gz < groups_z - 1, 1.0, 0.0)
    has_before_y = jnp.where(gy > 0, 1.0, 0.0)
    has_after_y = jnp.where(gy < groups_y - 1, 1.0, 0.0)
    mix = mix_ref[...]
    coef = coef_ref[...]
    expand = (lax.shift_right_logical(iota((256, C), 0), 3) == iota((256, C), 1)).astype(F32)
    gather = (lax.shift_right_logical(iota((C, 256), 1), 3) == iota((C, 256), 0)).astype(F32)
    row_y = lax.bitwise_and(iota((256, 256), 0), 7)
    col_y = lax.bitwise_and(iota((256, 256), 1), 7)

    for halo in halos:
        halo.wait_recv()
    def outside(which):
        if which < 2:
            return plane(hz_recv.at[which], 0, 256) * (has_before_z, has_after_z)[which]
        return plane(hy_recv.at[which - 2], 0, ZL * C) * (has_before_y, has_after_y)[which - 2]

    before_z, after_z, before_y, after_y = [outside(which) for which in range(4)]
    planes = [before_z] + [plane(slo2, z * 256, 256) for z in range(ZL)] + [after_z]
    for z in range(ZL):
        right = split(plane(inp2, z * 256, 256))
        left = split(
            jnp.concatenate(
                [planes[z + 1], planes[z], planes[z + 2],
                 before_y[z * C : (z + 1) * C], after_y[z * C : (z + 1) * C]], axis=0,
            )
        )
        term = dot3(left, right, NT)
        gram = term if z == 0 else gram + term
    gram_0, gram_up, gram_down = gram[0:256], gram[256:512], gram[512:768]
    same = row_y == col_y
    pieces = jnp.concatenate(
        [
            jnp.where(same, gram_0, 0.0),
            jnp.where(col_y == row_y + 1, gram_0, 0.0),
            jnp.where(col_y == row_y - 1, gram_0, 0.0),
            jnp.where(same, gram_up, 0.0),
            jnp.where(same, gram_down, 0.0),
        ],
        axis=1,
    )
    summed = dot3(gather, pieces, NN)
    edge_y = col_y[0:C]
    sums = [summed[:, j * 256 : (j + 1) * 256] for j in range(5)]
    sums[1] = sums[1] + jnp.where(edge_y == 0, gram[768 : 768 + C], 0.0)
    sums[2] = sums[2] + jnp.where(edge_y == YL - 1, gram[768 + C : 768 + 2 * C], 0.0)
    moments = [dot3(part, expand, NN) for part in sums]
    red_send[...] = jnp.zeros_like(red_send)
    local_mix = coef[0:1, :] * moments[0]
    for j in range(1, 5):
        local_mix = local_mix + coef[j : j + 1, :] * moments[j]
    red_send[0, 0:C, 0:C] = local_mix
    for j in range(5):
        red_send[0, C + j : C + j + 1, 0:C] = jnp.sum(mix * moments[j], axis=0, keepdims=True)

    def place(phase):
        stride, size = phases[phase]
        if stride == 0:
            return size, gz
        return size, lax.rem(gy // stride, size)

    def piece(phase, i, inward):
        stride, _ = phases[phase]
        size, mine = place(phase)
        peer = lax.rem(mine + i, size)
        slot = peer if inward else mine
        device = (peer, gy) if stride == 0 else (gz, gy + (peer - mine) * stride)
        return pltpu.make_async_remote_copy(
            red_send.at[phase], red_recv.at[phase, slot], sr.at[phase, i], rr.at[phase, slot],
            device_id=device, device_id_type=MESH,
        )

    def tree_send(phase):
        size, mine = place(phase)
        for i in range(1, size):
            piece(phase, i, False).start()
        red_recv[phase, mine] = red_send[phase]

    def tree_take(phase):
        size, _ = place(phase)
        for i in range(1, size):
            piece(phase, i, True).wait_recv()
        total = red_recv[phase, 0]
        for j in range(1, size):
            total = total + red_recv[phase, j]
        if phase + 1 < len(phases):
            red_send[phase + 1] = total
        else:
            red_sum[...] = total * (1.0 / 1024.0)

    tree_send(0)

    each(first_in, "wait_recv")
    received = rbuf[...].reshape(groups_y, 4, YL, LANES)
    received = jnp.concatenate(
        [received[:, part].reshape(groups_y * YL, LANES) for part in range(4)], axis=1
    )
    turned = dot3(wy_ref[...], received, NN)
    cos_part, sin_part = turned[0:32], turned[32:64]
    for field in range(2):
        re = slice(2 * field * LANES, (2 * field + 1) * LANES)
        im = slice((2 * field + 1) * LANES, (2 * field + 2) * LANES)
        zsend[:, re] = cos_part[:, re] + sin_part[:, im]
        zsend[:, im] = cos_part[:, im] - sin_part[:, re]
    for i in range(1, groups_z):
        across(zsend, zrecv, sz, rz, i, False).start()
    own = pl.ds(pl.multiple_of(gz * 8, 8), 8)
    zrecv[own, :] = zsend[own, :]
    tree_take(0)
    if len(phases) > 1:
        tree_send(1)
    for i in range(1, groups_z):
        across(zsend, zrecv, sz, rz, i, True).wait_recv()

    cos_z = [tw_ref[2 * k : 2 * k + 1, :] for k in range(4)]
    sin_z = [tw_ref[2 * k + 1 : 2 * k + 2, :] for k in range(4)]
    for field in range(2):
        base = 2 * field * LANES
        re = [zrecv[q * 8 : q * 8 + 8, base : base + LANES] for q in range(4)]
        im = [zrecv[q * 8 : q * 8 + 8, base + LANES : base + 2 * LANES] for q in range(4)]
        re, im = dft4(re, im, -1)
        for k in range(4):
            t_re, t_im = re[k], im[k]
            if k:
                t_re, t_im = turn(t_re, t_im, cos_z[k], sin_z[k], -1)
            f_re, f_im = dft4(
                [t_re] + [pltpu.roll(t_re, LANES - 32 * s, 1) for s in range(1, 4)],
                [t_im] + [pltpu.roll(t_im, LANES - 32 * s, 1) for s in range(1, 4)],
                -1,
            )
            for m in range(4):
                at = pl.ds((k + 4 * m) * 8, 8)
                if field == 0:
                    hin[0, at, :] = f_re[m]
                    hin[1, at, :] = f_im[m]
                else:
                    hsl[0, at, :] = f_re[m] * (1.0 / cell_total)
                    hsl[1, at, :] = f_im[m] * (1.0 / cell_total)
    for part in range(2):
        hslt[part] = hsl[part].T[0:C, :]

    load(3, wts_hbm, wts).wait()

    def dual_step(kz, carry):
        shift = lax.rem(NK - kz * 8, NK)
        slope_re = pltpu.roll(hslt[0], shift, 1)
        slope_im = pltpu.roll(hslt[1], shift, 1)
        for j in range(8):
            k = kz * 8 + j
            s_re = jnp.broadcast_to(slope_re[:, j : j + 1], (C, C))
            s_im = jnp.broadcast_to(slope_im[:, j : j + 1], (C, C))
            w_re, w_im = wts[0, k], wts[1, k]
            dual[0, pl.ds(k, 1), 0:C] = jnp.sum(w_re * s_re + w_im * s_im, axis=0, keepdims=True)
            dual[1, pl.ds(k, 1), 0:C] = jnp.sum(w_re * s_im - w_im * s_re, axis=0, keepdims=True)
        return carry

    lax.fori_loop(0, 16, dual_step, 0)

    block = lax.shift_right_logical(iota((8, LANES), 1), 5)
    v_re, v_im = [], []
    for k in range(4):
        u_re, u_im = dft4(
            [dual[0, pl.ds((k + 4 * m) * 8, 8), :] for m in range(4)],
            [dual[1, pl.ds((k + 4 * m) * 8, 8), :] for m in range(4)],
            1,
        )
        packed = []
        for u in (u_re, u_im):
            value = u[0]
            for s in range(1, 4):
                value = jnp.where(block == s, pltpu.roll(u[s], 32 * s, 1), value)
            packed.append(value)
        if k:
            packed = turn(packed[0], packed[1], cos_z[k], sin_z[k], 1)
        v_re.append(packed[0])
        v_im.append(packed[1])
    v_re, v_im = dft4(v_re, v_im, 1)
    for q in range(4):
        zsend2[q * 8 : q * 8 + 8, 0:LANES] = v_re[q]
        zsend2[q * 8 : q * 8 + 8, LANES : 2 * LANES] = v_im[q]
    for i in range(1, groups_z):
        across(zsend2, zrecv2, sz2, rz2, i, False).start()
    zrecv2[own, :] = zsend2[own, :]
    if len(phases) > 1:
        tree_take(1)
    if len(phases) > 2:
        tree_send(2)
    for i in range(1, groups_z):
        across(zsend2, zrecv2, sz2, rz2, i, True).wait_recv()

    upper = zrecv2[...]
    lower = jnp.concatenate([-upper[:, LANES:], upper[:, :LANES]], axis=1)
    back = dot3(wyt_ref[...], jnp.concatenate([upper, lower], axis=0), NN)
    sbuf2[...] = jnp.concatenate(
        [
            back[:, part * LANES : (part + 1) * LANES].reshape(groups_y, 1, YL, LANES)
            for part in range(2)
        ],
        axis=1,
    ).reshape(groups_y * 2 * YL, LANES)
    each(second, "start")
    own_rows = pltpu.make_async_copy(rows(sbuf2, gy, 2 * YL), rows(lines_out, gy, 2 * YL), out_sem.at[0])
    own_rows.start()
    if len(phases) > 2:
        tree_take(2)
    if len(phases) > 3:
        tree_send(3)

    coef_rows = dot3(expand, coef, NT)
    coef_col = [coef_rows[:, j : j + 1] for j in range(5)]
    full = dot3(dot3(expand, mix, NT), expand, NT)
    weight = jnp.concatenate(
        [
            full
            * (
                jnp.where(same, coef_col[0], 0.0)
                + jnp.where(row_y == col_y + 1, coef_col[1], 0.0)
                + jnp.where(row_y == col_y - 1, coef_col[2], 0.0)
            ),
            jnp.where(same, full, 0.0),
        ],
        axis=0,
    )
    weight = split(weight)
    for z in range(ZL):
        both = dot3(weight, plane(slo2, z * 256, 256), NN)
        put_plane(sten, z * 256, both[0:256])
        hid[z + 1] = both[256:512]
    plain = (weight[0][256:512], weight[1][256:512])
    hid[0] = dot3(plain, outside(0), NN)
    hid[5] = dot3(plain, outside(1), NN)
    for z in range(ZL):
        total = plane(sten, z * 256, 256) + coef_col[3] * hid[z] + coef_col[4] * hid[z + 2]
        put_plane(sten, z * 256, total)
    coef_small = dot3(
        (iota((C, C), 0) == iota((C, C), 1)).astype(F32), coef, NT
    )
    edges = jnp.concatenate(
        [outside(2)[z * C : (z + 1) * C] for z in range(ZL)]
        + [outside(3)[z * C : (z + 1) * C] for z in range(ZL)],
        axis=1,
    )
    edge_hidden = dot3(mix, edges, TN)
    for z in range(ZL):
        for side, y in enumerate((0, YL - 1)):
            at = pl.ds(z * 256 + y, C, stride=YL)
            for half in range(2):
                column = (side * ZL + z) * NX + half * LANES
                sten[half, at, :] = (
                    sten[half, at, :]
                    + coef_small[:, 1 + side : 2 + side]
                    * edge_hidden[:, column : column + LANES]
                )
    outs = [
        pltpu.make_async_copy(sten, sten_out, out_sem.at[1]),
        pltpu.make_async_copy(hin, hin_out, out_sem.at[2]),
        pltpu.make_async_copy(hslt, hsl_out, out_sem.at[3]),
    ]
    for out in outs:
        out.start()
    if len(phases) > 3:
        tree_take(3)
    total_out = pltpu.make_async_copy(red_sum, red_out, out_sem.at[4])
    total_out.start()

    each(second_in, "wait_recv")
    own_rows.wait()
    for out in outs:
        out.wait()
    total_out.wait()
    each(first, "wait_send")
    each(second, "wait_send")
    for halo in halos:
        halo.wait_send()
    for i in range(1, groups_z):
        across(zsend, zrecv, sz, rz, i, False).wait_send()
        across(zsend2, zrecv2, sz2, rz2, i, False).wait_send()
    for phase in range(len(phases)):
        for i in range(1, place(phase)[0]):
            piece(phase, i, False).wait_send()


def result_kernel(
    lines, sten, hin, hsl, red, wx_ref,
    grad_input, grad_spectral, grad_mix, grad_coef,
    cells, spectral, out_sem,
):
    modes_x = wx_ref.shape[0] // 2

    def part(kz):
        at = pl.ds(kz * 8, 8)
        return pltpu.make_async_copy(
            spectral.at[:, at], grad_spectral.at[:, at], out_sem.at[kz]
        )

    def outer_step(kz, carry):
        shift = lax.rem(NK - kz * 8, NK)
        slope_re = pltpu.roll(hsl[0], shift, 1)
        slope_im = pltpu.roll(hsl[1], shift, 1)
        for j in range(8):
            k = kz * 8 + j
            s_re = jnp.broadcast_to(slope_re[:, j : j + 1], (C, C))
            s_im = jnp.broadcast_to(slope_im[:, j : j + 1], (C, C))
            i_re = hin[0, pl.ds(k, 1), 0:C]
            i_im = hin[1, pl.ds(k, 1), 0:C]
            spectral[0, k] = s_re * i_re + s_im * i_im
            spectral[1, k] = s_im * i_re - s_re * i_im
        part(kz).start()
        return carry

    lax.fori_loop(0, 16, outer_step, 0)
    grad_mix[...] = red[0:C, 0:C]
    grad_coef[...] = red[C : C + 5, 0:C]
    spread = jnp.concatenate(
        [
            jnp.concatenate(
                [lines[pl.ds(part * YL + y, modes_x, stride=2 * YL), :] for y in range(YL)], axis=1
            )
            for part in range(2)
        ],
        axis=0,
    )
    result = dot3(spread, wx_ref[...], TN)
    for y in range(YL):
        for half in range(2):
            cells[half, pl.ds(y, LANES, stride=YL), :] = result[
                y * LANES : (y + 1) * LANES, half * LANES : (half + 1) * LANES
            ]
    for z in range(ZL):
        total = plane(cells, z * 256, 256) + plane(sten, z * 256, 256)
        grad_input[:, z] = total.reshape(C, YL, NX)

    def finish(kz, carry):
        part(kz).wait()
        return carry

    lax.fori_loop(0, 16, finish, 0)


def per_device(input_field, pre_activation, cotangent, spectral_weights, mix_weights, coefficients):
    groups_y = lax.axis_size("gy")
    groups_z = lax.axis_size("gz")
    grid_y = YL * groups_y
    modes_x = groups_y
    cell_total = NX * grid_y * ZL * groups_z
    phases = ((0, groups_z), (1, 4), (4, 2), (8, 4)) if groups_y == 32 else ((0, groups_z), (1, 4))
    rows_y = groups_y * YL
    cos_x, sin_x = table(NX, modes_x)
    cos_y, sin_y = table(grid_y, 32)
    wx = np.concatenate([cos_x, -sin_x]).astype(np.float32)
    wy = np.concatenate([cos_y, sin_y]).astype(np.float32)
    cell = np.arange(LANES) // C
    tw = np.stack(
        [fn(2.0 * math.pi * k * cell / 16.0) for k in range(4) for fn in (np.cos, np.sin)]
    ).astype(np.float32)
    weights = spectral_weights.reshape(2, NK, C, C)
    vmem = pl.BlockSpec(memory_space=pltpu.VMEM)
    anyspace = pl.BlockSpec(memory_space=pl.ANY)
    sds = jax.ShapeDtypeStruct
    dma = pltpu.SemaphoreType.DMA
    lines, sten, hin, hsl, red = pl.pallas_call(
        functools.partial(exchange_kernel, groups_y, groups_z, phases, cell_total),
        name="exchange",
        out_shape=(
            sds((2 * rows_y, LANES), F32),
            sds((2, ZL * 256, LANES), F32),
            sds((2, NK, LANES), F32),
            sds((2, C, NK), F32),
            sds((40, LANES), F32),
        ),
        in_specs=[anyspace] * 4 + [vmem] * 6,
        out_specs=(anyspace,) * 5,
        scratch_shapes=[
            pltpu.VMEM((C, ZL, YL, NX), F32),
            pltpu.VMEM((C, ZL, YL, NX), F32),
            pltpu.VMEM((C, ZL, YL, NX), F32),
            pltpu.VMEM((2, NK, C, C), F32),
            pltpu.VMEM((2, ZL * 256, LANES), F32),
            pltpu.VMEM((2, ZL * 256, LANES), F32),
            pltpu.VMEM((4 * rows_y, LANES), F32),
            pltpu.VMEM((4 * rows_y, LANES), F32),
            pltpu.VMEM((32, 4 * LANES), F32),
            pltpu.VMEM((32, 4 * LANES), F32),
            pltpu.VMEM((32, 2 * LANES), F32),
            pltpu.VMEM((32, 2 * LANES), F32),
            pltpu.VMEM((2 * rows_y, LANES), F32),
            pltpu.VMEM((2, 2, ZL * C, LANES), F32),
            pltpu.VMEM((2, 2, ZL * C, LANES), F32),
            pltpu.VMEM((2, 2, 256, LANES), F32),
            pltpu.VMEM((6, 256, NX), F32),
            pltpu.VMEM((2, ZL * 256, LANES), F32),
            pltpu.VMEM((2, NK, LANES), F32),
            pltpu.VMEM((2, NK, LANES), F32),
            pltpu.VMEM((2, C, NK), F32),
            pltpu.VMEM((2, NK, LANES), F32),
            pltpu.VMEM((len(phases), 40, LANES), F32),
            pltpu.VMEM((len(phases), 4, 40, LANES), F32),
            pltpu.VMEM((40, LANES), F32),
            dma((4,)),
            dma((groups_y,)), dma((groups_y,)), dma((groups_y,)), dma((groups_y,)),
            dma((groups_z,)), dma((groups_z,)), dma((groups_z,)), dma((groups_z,)),
            dma((4,)), dma((4,)),
            dma((len(phases), 4)), dma((len(phases), 4)),
            dma((5,)),
        ],
        compiler_params=pltpu.CompilerParams(collective_id=0, has_side_effects=True),
    )(
        input_field, pre_activation, cotangent, weights, mix_weights, coefficients,
        jnp.asarray(wx), jnp.asarray(wy), jnp.asarray(wy.T.copy()), jnp.asarray(tw),
    )
    grad_input, grad_spectral, grad_mix, grad_coef = pl.pallas_call(
        result_kernel,
        name="result",
        out_shape=(
            sds((C, ZL, YL, NX), F32),
            sds((2, NK, C, C), F32),
            sds((C, C), F32),
            sds((5, C), F32),
        ),
        in_specs=[vmem] * 6,
        out_specs=(vmem, anyspace, vmem, vmem),
        scratch_shapes=[
            pltpu.VMEM((2, ZL * 256, LANES), F32),
            pltpu.VMEM((2, NK, C, C), F32),
            dma((16,)),
        ],
    )(lines, sten, hin, hsl, red, jnp.asarray(wx))
    return (grad_input, grad_spectral.reshape(spectral_weights.shape), grad_mix, grad_coef)


def solution(mesh):
    in_specs = (
        P(None, "gz", "gy", None),
        P(None, "gz", "gy", None),
        P(None, "gz", "gy", None),
        P(None, None, "gz", "gy", None, None),
        P(),
        P(),
    )
    out_specs = (P(None, "gz", "gy", None), P(None, None, "gz", "gy", None, None), P(), P())
    return jax.shard_map(
        per_device, mesh=mesh, in_specs=in_specs, out_specs=out_specs, check_vma=False
    )
```

profile of v0, /device:TPU:1, one launch (start us, length us, event | category | flops | bytes accessed | tf_op | source)
XLA Modules:
  0.0 55.8 jit_solution(15494598740700057128)
XLA Ops:
  0.6 48.3 %exchange.1 = (f32[512,128]{1,0:T(8,128)}, f32[2,1024,128]{2,1,0:T(8,128)}, f32[2,128,128]{2,1,0:T(8,128)}, f32[2,32,128]{2,1,0:T(8,128)}, f32[40,128]{1,0:T(8,128)}) custom-call(f32[32,4,8,256]{3,2,1,0:T(8,128)} %inp_hbm.1, f32[32,4,8,256]{3,2,1,0:T(8,128)} %pre_hbm.1, f32[32,4,8,256]{3,2,1,0:T(8,128)} %cot_hbm.1, f32[2,128,32,32]{3,2,1,0:T(8,128)} %bitcast.4, ...), custom_call_target="tpu_custom_call" | custom-call | tf_op jit(solution)/shard_map/exchange/pallas_call | solution.py:594
  49.0 6.9 %result.1 = (f32[32,4,8,256]{3,2,1,0:T(8,128)}, f32[2,128,32,32]{3,2,1,0:T(8,128)}, f32[32,32]{1,0:T(8,128)}, f32[5,32]{1,0:T(8,128)}) custom-call(f32[512,128]{1,0:T(8,128)} %get-tuple-element.13.lines, f32[2,1024,128]{2,1,0:T(8,128)} %get-tuple-element.14.sten, f32[2,128,128]{2,1,0:T(8,128)} %get-tuple-element.15.hin, ...), custom_call_target="tpu_custom_call" | custom-call | tf_op jit(solution)/shard_map/result/pallas_call | solution.py:644
where the time goes:
time: 56 us; the launch traced here: 55.8 us
  Pallas kernels  55.2 us (99%)
  between operations  0.64 us (1%)
    pallas_call x1, Pallas kernels, per_device(): pl.pallas_call(functools.partial(exchange_kernel, groups_y, groups_z, pha...  48.3 us
    pallas_call x1, Pallas kernels, per_device(): pl.pallas_call(result_kernel, name='result', out_shape=(sds((C, ZL, YL, N...  6.85 us

commit v1 on v0

--- a/solution.py
+++ b/solution.py
@@ -81,6 +81,19 @@
         ref[half, pl.ds(start, value.shape[0]), :] = value[:, half * LANES : (half + 1) * LANES]
 
 
+def offsets(groups_y):
+    sizes = (4, 2, 4) if groups_y == 32 else (4,)
+    result = []
+    for i in range(1, groups_y):
+        moves, rest = [], i
+        for size in sizes:
+            moves.append((size, rest % size))
+            rest //= size
+        hops = sum(min(m, n - m) * (2 if n == 2 else 1) for n, m in moves)
+        result.append((-hops, tuple(moves)))
+    return [moves for _, moves in sorted(result)]
+
+
 def iota(shape, axis):
     return lax.broadcasted_iota(jnp.int32, shape, axis)
 
@@ -88,9 +101,9 @@
 def exchange_kernel(
     groups_y, groups_z, phases, cell_total,
     inp_hbm, pre_hbm, cot_hbm, wts_hbm, mix_ref, coef_ref, wx_ref, wy_ref, wyt_ref, tw_ref,
-    lines_out, sten_out, hin_out, hsl_out, red_out,
+    lines_out, sten, spectral, red_sum,
     inp4, pre4, cot4, wts, inp2, slo2, sbuf, rbuf, zsend, zrecv, zsend2, zrecv2, sbuf2,
-    hy_send, hy_recv, hz_recv, hid, sten, hin, hsl, hslt, dual, red_send, red_recv, red_sum,
+    hy_send, hy_recv, hz_recv, hid, gram, hin, hsl, hslt, dual, red_send, red_recv,
     load_sem, s1, r1, s2, r2, sz, rz, sz2, rz2, hs_sem, hr_sem, sr, rr, out_sem,
 ):
     gz = lax.axis_index("gz")
@@ -165,8 +178,17 @@
     def rows(ref, index, size=YL):
         return ref.at[pl.ds(pl.multiple_of(index * size, size), size), :]
 
+    def partner(i):
+        if isinstance(i, tuple):
+            digits, stride, peer = gy, 1, 0
+            for size, move in i:
+                peer = peer + lax.rem(lax.rem(digits, size) + move, size) * stride
+                digits, stride = digits // size, stride * size
+            return peer
+        return lax.rem(gy + i, groups_y)
+
     def first(i):
-        peer = lax.rem(gy + i, groups_y)
+        peer = partner(i)
         return pltpu.make_async_remote_copy(
             rows(sbuf, peer, 4 * YL), rows(rbuf, gy, 4 * YL), s1.at[peer], r1.at[gy],
             device_id=(gz, peer), device_id_type=MESH,
@@ -180,7 +202,7 @@
         )
 
     def second(i):
-        peer = lax.rem(gy + i, groups_y)
+        peer = partner(i)
         return pltpu.make_async_remote_copy(
             rows(sbuf2, peer, 2 * YL), rows(lines_out, gy, 2 * YL), s2.at[peer], r2.at[gy],
             device_id=(gz, peer), device_id_type=MESH,
@@ -201,6 +223,10 @@
             device_id=(peer, gy), device_id_type=MESH,
         )
 
+    def each_far(make):
+        for i in offsets(groups_y):
+            make(i).start()
+
     def each(make, action):
         def body(i, carry):
             getattr(make(i), action)()
@@ -208,32 +234,33 @@
 
         lax.fori_loop(1, groups_y, body, 0)
 
-    each(first, "start")
+    each_far(first)
     own_lines = pl.ds(pl.multiple_of(gy * 4 * YL, 4 * YL), 4 * YL)
     rbuf[own_lines, :] = sbuf[own_lines, :]
 
     next_z, prev_z = lax.rem(gz + 1, groups_z), lax.rem(gz + groups_z - 1, groups_z)
     next_y, prev_y = lax.rem(gy + 1, groups_y), lax.rem(gy + groups_y - 1, groups_y)
     halos = []
-    for i, (source, target, device) in enumerate(
+    for i, (source, target, device, sends, takes) in enumerate(
         (
-            (slo2.at[:, pl.ds(3 * 256, 256), :], hz_recv.at[0], (next_z, gy)),
-            (slo2.at[:, pl.ds(0, 256), :], hz_recv.at[1], (prev_z, gy)),
-            (hy_send.at[0], hy_recv.at[0], (gz, next_y)),
-            (hy_send.at[1], hy_recv.at[1], (gz, prev_y)),
+            (slo2.at[:, pl.ds(3 * 256, 256), :], hz_recv.at[0], (next_z, gy),
+             gz < groups_z - 1, gz > 0),
+            (slo2.at[:, pl.ds(0, 256), :], hz_recv.at[1], (prev_z, gy),
+             gz > 0, gz < groups_z - 1),
+            (hy_send.at[0], hy_recv.at[0], (gz, next_y), gy < groups_y - 1, gy > 0),
+            (hy_send.at[1], hy_recv.at[1], (gz, prev_y), gy > 0, gy < groups_y - 1),
         )
     ):
-        halos.append(
-            pltpu.make_async_remote_copy(
-                source, target, hs_sem.at[i], hr_sem.at[i], device_id=device, device_id_type=MESH
-            )
-        )
-        halos[-1].start()
-
-    has_before_z = jnp.where(gz > 0, 1.0, 0.0)
-    has_after_z = jnp.where(gz < groups_z - 1, 1.0, 0.0)
-    has_before_y = jnp.where(gy > 0, 1.0, 0.0)
-    has_after_y = jnp.where(gy < groups_y - 1, 1.0, 0.0)
+        copy = pltpu.make_async_remote_copy(
+            source, target, hs_sem.at[i], hr_sem.at[i], device_id=device, device_id_type=MESH
+        )
+        halos.append((copy, sends, takes))
+        pl.when(sends)(copy.start)
+
+        @pl.when(jnp.logical_not(takes))
+        def _():
+            target[...] = jnp.zeros(target.shape, F32)
+
     mix = mix_ref[...]
     coef = coef_ref[...]
     expand = (lax.shift_right_logical(iota((256, C), 0), 3) == iota((256, C), 1)).astype(F32)
@@ -241,50 +268,79 @@
     row_y = lax.bitwise_and(iota((256, 256), 0), 7)
     col_y = lax.bitwise_and(iota((256, 256), 1), 7)
 
-    for halo in halos:
-        halo.wait_recv()
     def outside(which):
         if which < 2:
-            return plane(hz_recv.at[which], 0, 256) * (has_before_z, has_after_z)[which]
-        return plane(hy_recv.at[which - 2], 0, ZL * C) * (has_before_y, has_after_y)[which - 2]
-
-    before_z, after_z, before_y, after_y = [outside(which) for which in range(4)]
-    planes = [before_z] + [plane(slo2, z * 256, 256) for z in range(ZL)] + [after_z]
+            return plane(hz_recv.at[which], 0, 256)
+        return plane(hy_recv.at[which - 2], 0, ZL * C)
+
+    def gram_of(left, z):
+        return dot3(left, split(plane(inp2, z * 256, 256)), NT)
+
+    same = row_y == col_y
+    coef_rows = dot3(expand, coef, NT)
+    coef_col = [coef_rows[:, j : j + 1] for j in range(5)]
+    full = dot3(dot3(expand, mix, NT), expand, NT)
+    weight = jnp.concatenate(
+        [
+            full
+            * (
+                jnp.where(same, coef_col[0], 0.0)
+                + jnp.where(row_y == col_y + 1, coef_col[1], 0.0)
+                + jnp.where(row_y == col_y - 1, coef_col[2], 0.0)
+            ),
+            jnp.where(same, full, 0.0),
+        ],
+        axis=0,
+    )
+    weight = split(weight)
+    plain = (weight[0][256:512], weight[1][256:512])
     for z in range(ZL):
-        right = split(plane(inp2, z * 256, 256))
-        left = split(
-            jnp.concatenate(
-                [planes[z + 1], planes[z], planes[z + 2],
-                 before_y[z * C : (z + 1) * C], after_y[z * C : (z + 1) * C]], axis=0,
-            )
-        )
-        term = dot3(left, right, NT)
-        gram = term if z == 0 else gram + term
-    gram_0, gram_up, gram_down = gram[0:256], gram[256:512], gram[512:768]
-    same = row_y == col_y
-    pieces = jnp.concatenate(
-        [
-            jnp.where(same, gram_0, 0.0),
-            jnp.where(col_y == row_y + 1, gram_0, 0.0),
-            jnp.where(col_y == row_y - 1, gram_0, 0.0),
-            jnp.where(same, gram_up, 0.0),
-            jnp.where(same, gram_down, 0.0),
-        ],
-        axis=1,
-    )
-    summed = dot3(gather, pieces, NN)
-    edge_y = col_y[0:C]
-    sums = [summed[:, j * 256 : (j + 1) * 256] for j in range(5)]
-    sums[1] = sums[1] + jnp.where(edge_y == 0, gram[768 : 768 + C], 0.0)
-    sums[2] = sums[2] + jnp.where(edge_y == YL - 1, gram[768 + C : 768 + 2 * C], 0.0)
-    moments = [dot3(part, expand, NN) for part in sums]
-    red_send[...] = jnp.zeros_like(red_send)
-    local_mix = coef[0:1, :] * moments[0]
-    for j in range(1, 5):
-        local_mix = local_mix + coef[j : j + 1, :] * moments[j]
-    red_send[0, 0:C, 0:C] = local_mix
-    for j in range(5):
-        red_send[0, C + j : C + j + 1, 0:C] = jnp.sum(mix * moments[j], axis=0, keepdims=True)
+        both = dot3(weight, plane(slo2, z * 256, 256), NN)
+        put_plane(sten, z * 256, both[0:256])
+        hid[z + 1] = both[256:512]
+    own = [split(plane(slo2, z * 256, 256)) for z in range(ZL)]
+    for kind, shift in enumerate((0, -1, 1)):
+        total = None
+        for z in range(ZL):
+            if 0 <= z + shift < ZL:
+                term = gram_of(own[z + shift], z)
+                total = term if total is None else total + term
+        gram[kind] = total
+
+    def moments():
+        gram_0 = gram[0]
+        gram_up = gram[1] + gram_of(outside(0), 0)
+        gram_down = gram[2] + gram_of(outside(1), ZL - 1)
+        before_y, after_y = outside(2), outside(3)
+        edge = None
+        for z in range(ZL):
+            at = slice(z * C, (z + 1) * C)
+            term = gram_of(jnp.concatenate([before_y[at], after_y[at]], axis=0), z)
+            edge = term if z == 0 else edge + term
+        pieces = jnp.concatenate(
+            [
+                jnp.where(same, gram_0, 0.0),
+                jnp.where(col_y == row_y + 1, gram_0, 0.0),
+                jnp.where(col_y == row_y - 1, gram_0, 0.0),
+                jnp.where(same, gram_up, 0.0),
+                jnp.where(same, gram_down, 0.0),
+            ],
+            axis=1,
+        )
+        summed = dot3(gather, pieces, NN)
+        edge_y = col_y[0:C]
+        sums = [summed[:, j * 256 : (j + 1) * 256] for j in range(5)]
+        sums[1] = sums[1] + jnp.where(edge_y == 0, edge[0:C], 0.0)
+        sums[2] = sums[2] + jnp.where(edge_y == YL - 1, edge[C : 2 * C], 0.0)
+        every = dot3(jnp.concatenate(sums, axis=0), expand, NN)
+        parts = [every[j * C : (j + 1) * C] for j in range(5)]
+        red_send[0] = jnp.zeros((40, LANES), F32)
+        local_mix = coef[0:1, :] * parts[0]
+        for j in range(1, 5):
+            local_mix = local_mix + coef[j : j + 1, :] * parts[j]
+        red_send[0, 0:C, 0:C] = local_mix
+        for j in range(5):
+            red_send[0, C + j : C + j + 1, 0:C] = jnp.sum(mix * parts[j], axis=0, keepdims=True)
 
     def place(phase):
         stride, size = phases[phase]
@@ -320,8 +376,6 @@
             red_send[phase + 1] = total
         else:
             red_sum[...] = total * (1.0 / 1024.0)
-
-    tree_send(0)
 
     each(first_in, "wait_recv")
     received = rbuf[...].reshape(groups_y, 4, YL, LANES)
@@ -337,11 +391,8 @@
         zsend[:, im] = cos_part[:, im] - sin_part[:, re]
     for i in range(1, groups_z):
         across(zsend, zrecv, sz, rz, i, False).start()
-    own = pl.ds(pl.multiple_of(gz * 8, 8), 8)
-    zrecv[own, :] = zsend[own, :]
-    tree_take(0)
-    if len(phases) > 1:
-        tree_send(1)
+    mine = pl.ds(pl.multiple_of(gz * 8, 8), 8)
+    zrecv[mine, :] = zsend[mine, :]
     for i in range(1, groups_z):
         across(zsend, zrecv, sz, rz, i, True).wait_recv()
 
@@ -374,12 +425,12 @@
 
     load(3, wts_hbm, wts).wait()
 
-    def dual_step(kz, carry):
-        shift = lax.rem(NK - kz * 8, NK)
+    def dual_step(step, carry):
+        shift = lax.rem(NK - step * 32, NK)
         slope_re = pltpu.roll(hslt[0], shift, 1)
         slope_im = pltpu.roll(hslt[1], shift, 1)
-        for j in range(8):
-            k = kz * 8 + j
+        for j in range(32):
+            k = step * 32 + j
             s_re = jnp.broadcast_to(slope_re[:, j : j + 1], (C, C))
             s_im = jnp.broadcast_to(slope_im[:, j : j + 1], (C, C))
             w_re, w_im = wts[0, k], wts[1, k]
@@ -387,7 +438,7 @@
             dual[1, pl.ds(k, 1), 0:C] = jnp.sum(w_re * s_im - w_im * s_re, axis=0, keepdims=True)
         return carry
 
-    lax.fori_loop(0, 16, dual_step, 0)
+    lax.fori_loop(0, 4, dual_step, 0)
 
     block = lax.shift_right_logical(iota((8, LANES), 1), 5)
     v_re, v_im = [], []
@@ -413,11 +464,11 @@
         zsend2[q * 8 : q * 8 + 8, LANES : 2 * LANES] = v_im[q]
     for i in range(1, groups_z):
         across(zsend2, zrecv2, sz2, rz2, i, False).start()
-    zrecv2[own, :] = zsend2[own, :]
-    if len(phases) > 1:
-        tree_take(1)
-    if len(phases) > 2:
-        tree_send(2)
+    zrecv2[mine, :] = zsend2[mine, :]
+    for copy, _, takes in halos:
+        pl.when(takes)(copy.wait_recv)
+    moments()
+    tree_send(0)
     for i in range(1, groups_z):
         across(zsend2, zrecv2, sz2, rz2, i, True).wait_recv()
 
@@ -431,47 +482,40 @@
         ],
         axis=1,
     ).reshape(groups_y * 2 * YL, LANES)
-    each(second, "start")
+    each_far(second)
     own_rows = pltpu.make_async_copy(rows(sbuf2, gy, 2 * YL), rows(lines_out, gy, 2 * YL), out_sem.at[0])
     own_rows.start()
+
+    tree_take(0)
+    tree_send(1)
+
+    def outer_step(step, carry):
+        shift = lax.rem(NK - step * 32, NK)
+        slope_re = pltpu.roll(hslt[0], shift, 1)
+        slope_im = pltpu.roll(hslt[1], shift, 1)
+        for j in range(32):
+            k = step * 32 + j
+            s_re = jnp.broadcast_to(slope_re[:, j : j + 1], (C, C))
+            s_im = jnp.broadcast_to(slope_im[:, j : j + 1], (C, C))
+            i_re = hin[0, pl.ds(k, 1), 0:C]
+            i_im = hin[1, pl.ds(k, 1), 0:C]
+            spectral[0, k] = s_re * i_re + s_im * i_im
+            spectral[1, k] = s_im * i_re - s_re * i_im
+        return carry
+
+    lax.fori_loop(0, 4, outer_step, 0)
+    tree_take(1)
     if len(phases) > 2:
-        tree_take(2)
-    if len(phases) > 3:
-        tree_send(3)
-
-    coef_rows = dot3(expand, coef, NT)
-    coef_col = [coef_rows[:, j : j + 1] for j in range(5)]
-    full = dot3(dot3(expand, mix, NT), expand, NT)
-    weight = jnp.concatenate(
-        [
-            full
-            * (
-                jnp.where(same, coef_col[0], 0.0)
-                + jnp.where(row_y == col_y + 1, coef_col[1], 0.0)
-                + jnp.where(row_y == col_y - 1, coef_col[2], 0.0)
-            ),
-            jnp.where(same, full, 0.0),
-        ],
-        axis=0,
-    )
-    weight = split(weight)
-    for z in range(ZL):
-        both = dot3(weight, plane(slo2, z * 256, 256), NN)
-        put_plane(sten, z * 256, both[0:256])
-        hid[z + 1] = both[256:512]
-    plain = (weight[0][256:512], weight[1][256:512])
+        tree_send(2)
     hid[0] = dot3(plain, outside(0), NN)
     hid[5] = dot3(plain, outside(1), NN)
     for z in range(ZL):
         total = plane(sten, z * 256, 256) + coef_col[3] * hid[z] + coef_col[4] * hid[z + 2]
         put_plane(sten, z * 256, total)
-    coef_small = dot3(
-        (iota((C, C), 0) == iota((C, C), 1)).astype(F32), coef, NT
-    )
+    coef_small = dot3((iota((C, C), 0) == iota((C, C), 1)).astype(F32), coef, NT)
+    before_y, after_y = outside(2), outside(3)
     edges = jnp.concatenate(
-        [outside(2)[z * C : (z + 1) * C] for z in range(ZL)]
-        + [outside(3)[z * C : (z + 1) * C] for z in range(ZL)],
-        axis=1,
+        [side[z * C : (z + 1) * C] for side in (before_y, after_y) for z in range(ZL)], axis=1
     )
     edge_hidden = dot3(mix, edges, TN)
     for z in range(ZL):
@@ -484,27 +528,15 @@
                     + coef_small[:, 1 + side : 2 + side]
                     * edge_hidden[:, column : column + LANES]
                 )
-    outs = [
-        pltpu.make_async_copy(sten, sten_out, out_sem.at[1]),
-        pltpu.make_async_copy(hin, hin_out, out_sem.at[2]),
-        pltpu.make_async_copy(hslt, hsl_out, out_sem.at[3]),
-    ]
-    for out in outs:
-        out.start()
-    if len(phases) > 3:
-        tree_take(3)
-    total_out = pltpu.make_async_copy(red_sum, red_out, out_sem.at[4])
-    total_out.start()
+    if len(phases) > 2:
+        tree_take(2)
 
     each(second_in, "wait_recv")
     own_rows.wait()
-    for out in outs:
-        out.wait()
-    total_out.wait()
     each(first, "wait_send")
     each(second, "wait_send")
-    for halo in halos:
-        halo.wait_send()
+    for copy, sends, _ in halos:
+        pl.when(sends)(copy.wait_send)
     for i in range(1, groups_z):
         across(zsend, zrecv, sz, rz, i, False).wait_send()
         across(zsend2, zrecv2, sz2, rz2, i, False).wait_send()
@@ -514,34 +546,13 @@
 
 
 def result_kernel(
-    lines, sten, hin, hsl, red, wx_ref,
+    lines, sten, spectral, red, wx_ref,
     grad_input, grad_spectral, grad_mix, grad_coef,
-    cells, spectral, out_sem,
+    cells, out_sem,
 ):
     modes_x = wx_ref.shape[0] // 2
-
-    def part(kz):
-        at = pl.ds(kz * 8, 8)
-        return pltpu.make_async_copy(
-            spectral.at[:, at], grad_spectral.at[:, at], out_sem.at[kz]
-        )
-
-    def outer_step(kz, carry):
-        shift = lax.rem(NK - kz * 8, NK)
-        slope_re = pltpu.roll(hsl[0], shift, 1)
-        slope_im = pltpu.roll(hsl[1], shift, 1)
-        for j in range(8):
-            k = kz * 8 + j
-            s_re = jnp.broadcast_to(slope_re[:, j : j + 1], (C, C))
-            s_im = jnp.broadcast_to(slope_im[:, j : j + 1], (C, C))
-            i_re = hin[0, pl.ds(k, 1), 0:C]
-            i_im = hin[1, pl.ds(k, 1), 0:C]
-            spectral[0, k] = s_re * i_re + s_im * i_im
-            spectral[1, k] = s_im * i_re - s_re * i_im
-        part(kz).start()
-        return carry
-
-    lax.fori_loop(0, 16, outer_step, 0)
+    out = pltpu.make_async_copy(spectral, grad_spectral, out_sem.at[0])
+    out.start()
     grad_mix[...] = red[0:C, 0:C]
     grad_coef[...] = red[C : C + 5, 0:C]
     spread = jnp.concatenate(
@@ -562,12 +573,7 @@
     for z in range(ZL):
         total = plane(cells, z * 256, 256) + plane(sten, z * 256, 256)
         grad_input[:, z] = total.reshape(C, YL, NX)
-
-    def finish(kz, carry):
-        part(kz).wait()
-        return carry
-
-    lax.fori_loop(0, 16, finish, 0)
+    out.wait()
 
 
 def per_device(input_field, pre_activation, cotangent, spectral_weights, mix_weights, coefficients):
@@ -576,7 +582,7 @@
     grid_y = YL * groups_y
     modes_x = groups_y
     cell_total = NX * grid_y * ZL * groups_z
-    phases = ((0, groups_z), (1, 4), (4, 2), (8, 4)) if groups_y == 32 else ((0, groups_z), (1, 4))
+    phases = ((0, groups_z), (1, 8), (8, 4)) if groups_y == 32 else ((0, groups_z), (1, 4))
     rows_y = groups_y * YL
     cos_x, sin_x = table(NX, modes_x)
     cos_y, sin_y = table(grid_y, 32)
@@ -588,21 +594,20 @@
     ).astype(np.float32)
     weights = spectral_weights.reshape(2, NK, C, C)
     vmem = pl.BlockSpec(memory_space=pltpu.VMEM)
-    anyspace = pl.BlockSpec(memory_space=pl.ANY)
+    hbm = pl.BlockSpec(memory_space=pltpu.HBM)
     sds = jax.ShapeDtypeStruct
     dma = pltpu.SemaphoreType.DMA
-    lines, sten, hin, hsl, red = pl.pallas_call(
+    lines, sten, spectral, red = pl.pallas_call(
         functools.partial(exchange_kernel, groups_y, groups_z, phases, cell_total),
         name="exchange",
         out_shape=(
-            sds((2 * rows_y, LANES), F32),
-            sds((2, ZL * 256, LANES), F32),
-            sds((2, NK, LANES), F32),
-            sds((2, C, NK), F32),
-            sds((40, LANES), F32),
+            pltpu.VMEM((2 * rows_y, LANES), F32),
+            pltpu.VMEM((2, ZL * 256, LANES), F32),
+            pltpu.VMEM((2, NK, C, C), F32),
+            pltpu.VMEM((40, LANES), F32),
         ),
-        in_specs=[anyspace] * 4 + [vmem] * 6,
-        out_specs=(anyspace,) * 5,
+        in_specs=[hbm] * 4 + [vmem] * 6,
+        out_specs=(vmem,) * 4,
         scratch_shapes=[
             pltpu.VMEM((C, ZL, YL, NX), F32),
             pltpu.VMEM((C, ZL, YL, NX), F32),
@@ -621,25 +626,31 @@
             pltpu.VMEM((2, 2, ZL * C, LANES), F32),
             pltpu.VMEM((2, 2, 256, LANES), F32),
             pltpu.VMEM((6, 256, NX), F32),
-            pltpu.VMEM((2, ZL * 256, LANES), F32),
+            pltpu.VMEM((3, 256, 256), F32),
             pltpu.VMEM((2, NK, LANES), F32),
             pltpu.VMEM((2, NK, LANES), F32),
             pltpu.VMEM((2, C, NK), F32),
             pltpu.VMEM((2, NK, LANES), F32),
             pltpu.VMEM((len(phases), 40, LANES), F32),
-            pltpu.VMEM((len(phases), 4, 40, LANES), F32),
-            pltpu.VMEM((40, LANES), F32),
+            pltpu.VMEM((len(phases), 8, 40, LANES), F32),
             dma((4,)),
             dma((groups_y,)), dma((groups_y,)), dma((groups_y,)), dma((groups_y,)),
             dma((groups_z,)), dma((groups_z,)), dma((groups_z,)), dma((groups_z,)),
             dma((4,)), dma((4,)),
-            dma((len(phases), 4)), dma((len(phases), 4)),
-            dma((5,)),
+            dma((len(phases), 8)), dma((len(phases), 8)),
+            dma((1,)),
         ],
-        compiler_params=pltpu.CompilerParams(collective_id=0, has_side_effects=True),
+        compiler_params=pltpu.CompilerParams(
+            collective_id=0, has_side_effects=True, vmem_limit_bytes=40 << 20
+        ),
     )(
-        input_field, pre_activation, cotangent, weights, mix_weights, coefficients,
-        jnp.asarray(wx), jnp.asarray(wy), jnp.asarray(wy.T.copy()), jnp.asarray(tw),
+        *(
+            pltpu.with_memory_space_constraint(operand, pltpu.HBM)
+            for operand in (
+                input_field, pre_activation, cotangent, weights, mix_weights, coefficients,
+                jnp.asarray(wx), jnp.asarray(wy), jnp.asarray(wy.T.copy()), jnp.asarray(tw),
+            )
+        )
     )
     grad_input, grad_spectral, grad_mix, grad_coef = pl.pallas_call(
         result_kernel,
@@ -650,14 +661,14 @@
             sds((C, C), F32),
             sds((5, C), F32),
         ),
-        in_specs=[vmem] * 6,
-        out_specs=(vmem, anyspace, vmem, vmem),
+        in_specs=[vmem] * 5,
+        out_specs=(vmem, hbm, vmem, vmem),
         scratch_shapes=[
             pltpu.VMEM((2, ZL * 256, LANES), F32),
-            pltpu.VMEM((2, NK, C, C), F32),
-            dma((16,)),
+            dma((1,)),
         ],
-    )(lines, sten, hin, hsl, red, jnp.asarray(wx))
+        compiler_params=pltpu.CompilerParams(vmem_limit_bytes=24 << 20),
+    )(lines, sten, spectral, red, jnp.asarray(wx))
     return (grad_input, grad_spectral.reshape(spectral_weights.shape), grad_mix, grad_coef)
 
 

time: 56 us -> 47.9 us (0.86); the launches traced: 55.8 us -> 47 us
  Pallas kernels: 55.2 us -> 46.4 us
    pallas_call x1, Pallas kernels: 48.3 us -> 43.3 us  [per_device(): pl.pallas_call(functools.partial(exchange_kernel, groups_y, groups_z, pha...]
    pallas_call x1, Pallas kernels: 6.85 us -> 3.05 us  [per_device(): pl.pallas_call(result_kernel, name='result', out_shape=(sds((C, ZL, YL, N...]
where the time goes in v1:
time: 47.9 us; the launch traced here: 47 us
  Pallas kernels  46.4 us (97%)
  between operations  0.66 us (1%)
    pallas_call x1, Pallas kernels, per_device(): pl.pallas_call(functools.partial(exchange_kernel, groups_y, groups_z, pha...  43.3 us
    pallas_call x1, Pallas kernels, per_device(): pl.pallas_call(result_kernel, name='result', out_shape=(sds((C, ZL, YL, N...  3.05 us

profile of v1, /device:TPU:1, one launch (start us, length us, event | category | flops | bytes accessed | tf_op | source)
XLA Modules:
  0.0 47.0 jit_solution(18317068138999523777)
XLA Ops:
  0.6 0.0 copy-start
  0.6 43.3 %exchange.1 = (f32[512,128]{1,0:T(8,128)S(1)}, f32[2,1024,128]{2,1,0:T(8,128)S(1)}, f32[2,128,32,32]{3,2,1,0:T(8,128)S(1)}, f32[40,128]{1,0:T(8,128)S(1)}) custom-call(f32[32,4,8,256]{3,2,1,0:T(8,128)} %inp_hbm.1, f32[32,4,8,256]{3,2,1,0:T(8,128)} %pre_hbm.1, f32[32,4,8,256]{3,2,1,0:T(8,128)} %cot_hbm.1, f32[2,128,32,32]{3,2,1,0:T(8,128)} %bitcast.4, ...), custom_call_target="tpu_custom_call" | custom-call | tf_op jit(solution)/shard_map/exchange/pallas_call | solution.py:600
  44.0 0.0 copy-done
  44.0 3.0 %result.1 = (f32[32,4,8,256]{3,2,1,0:T(8,128)}, f32[2,128,32,32]{3,2,1,0:T(8,128)}, f32[32,32]{1,0:T(8,128)}, f32[5,32]{1,0:T(8,128)}) custom-call(f32[512,128]{1,0:T(8,128)S(1)} %get-tuple-element.12.lines, f32[2,1024,128]{2,1,0:T(8,128)S(1)} %get-tuple-element.13.sten, f32[2,128,32,32]{3,2,1,0:T(8,128)S(1)} %get-tuple-element.14.spectral, ...), custom_call_target="tpu_custom_call" | custom-call | tf_op jit(solution)/shard_map/result/pallas_call | solution.py:655
Async XLA Ops:
  0.6 43.3 %copy-start = (f32[64,256]{1,0:T(8,128)S(1)}, f32[64,256]{1,0:T(8,128)}, u32[]{:S(2)}) copy-start(f32[64,256]{1,0:T(8,128)} %constant.8.clone.wx_ref) | copy-start | bytes 196612

commit v2 on v1

--- a/solution.py
+++ b/solution.py
@@ -100,9 +100,9 @@
 
 def exchange_kernel(
     groups_y, groups_z, phases, cell_total,
-    inp_hbm, pre_hbm, cot_hbm, wts_hbm, mix_ref, coef_ref, wx_ref, wy_ref, wyt_ref, tw_ref,
+    inp_hbm, pre_hbm, cot_hbm, wts_hbm, mix_hbm, coef_hbm, wx_hbm, wy_hbm, wyt_hbm, tw_hbm,
     lines_out, sten, spectral, red_sum,
-    inp4, pre4, cot4, wts, inp2, slo2, sbuf, rbuf, zsend, zrecv, zsend2, zrecv2, sbuf2,
+    mix_ref, coef_ref, wx_ref, wy_ref, wyt_ref, tw_ref, inp4, pre4, cot4, wts, inp2, slo2, sbuf, rbuf, zsend, zrecv, zsend2, zrecv2, sbuf2,
     hy_send, hy_recv, hz_recv, hid, gram, hin, hsl, hslt, dual, red_send, red_recv,
     load_sem, s1, r1, s2, r2, sz, rz, sz2, rz2, hs_sem, hr_sem, sr, rr, out_sem,
 ):
@@ -113,21 +113,38 @@
     def load(i, src, dst):
         return pltpu.make_async_copy(src, dst, load_sem.at[i])
 
-    load(0, inp_hbm, inp4).start()
-    load(1, pre_hbm, pre4).start()
-    load(2, cot_hbm, cot4).start()
-
     barrier = pltpu.get_barrier_semaphore()
 
-    def greet(i, carry):
-        peer = lax.rem(gy + i, groups_y)
-        pl.semaphore_signal(barrier, inc=1, device_id=(gz, peer), device_id_type=MESH)
-        return carry
-
-    lax.fori_loop(1, groups_y, greet, 0)
+    def partner(i):
+        if isinstance(i, tuple):
+            digits, stride, peer = gy, 1, 0
+            for size, move in i:
+                peer = peer + lax.rem(lax.rem(digits, size) + move, size) * stride
+                digits, stride = digits // size, stride * size
+            return peer
+        return lax.rem(gy + i, groups_y)
+
+    for i in offsets(groups_y):
+        pl.semaphore_signal(barrier, inc=1, device_id=(gz, partner(i)), device_id_type=MESH)
     for i in range(1, groups_z):
         peer = lax.rem(gz + i, groups_z)
         pl.semaphore_signal(barrier, inc=1, device_id=(peer, gy), device_id_type=MESH)
+    loads = [
+        load(0, inp_hbm, inp4),
+        load(6, wx_hbm, wx_ref),
+        load(1, pre_hbm, pre4),
+        load(2, cot_hbm, cot4),
+    ]
+    small = [
+        load(4, mix_hbm, mix_ref),
+        load(5, coef_hbm, coef_ref),
+        load(7, wy_hbm, wy_ref),
+        load(8, wyt_hbm, wyt_ref),
+        load(9, tw_hbm, tw_ref),
+    ]
+    for copy in loads + small:
+        copy.start()
+    loads[1].wait()
 
     wx = split(wx_ref[...])
 
@@ -148,12 +165,12 @@
                     result[part * modes_x : (part + 1) * modes_x, y * LANES : (y + 1) * LANES]
                 )
 
-    load(0, inp_hbm, inp4).wait()
+    loads[0].wait()
     for z in range(ZL):
         put_plane(inp2, z * 256, inp4[:, z].reshape(256, NX))
     along_x(inp2, 0)
-    load(1, pre_hbm, pre4).wait()
-    load(2, cot_hbm, cot4).wait()
+    loads[2].wait()
+    loads[3].wait()
     load(3, wts_hbm, wts).start()
 
     def slope_step(step, carry):
@@ -177,15 +194,6 @@
 
     def rows(ref, index, size=YL):
         return ref.at[pl.ds(pl.multiple_of(index * size, size), size), :]
-
-    def partner(i):
-        if isinstance(i, tuple):
-            digits, stride, peer = gy, 1, 0
-            for size, move in i:
-                peer = peer + lax.rem(lax.rem(digits, size) + move, size) * stride
-                digits, stride = digits // size, stride * size
-            return peer
-        return lax.rem(gy + i, groups_y)
 
     def first(i):
         peer = partner(i)
@@ -261,6 +269,8 @@
         def _():
             target[...] = jnp.zeros(target.shape, F32)
 
+    for copy in small:
+        copy.wait()
     mix = mix_ref[...]
     coef = coef_ref[...]
     expand = (lax.shift_right_logical(iota((256, C), 0), 3) == iota((256, C), 1)).astype(F32)
@@ -334,13 +344,16 @@
         sums[2] = sums[2] + jnp.where(edge_y == YL - 1, edge[C : 2 * C], 0.0)
         every = dot3(jnp.concatenate(sums, axis=0), expand, NN)
         parts = [every[j * C : (j + 1) * C] for j in range(5)]
-        red_send[0] = jnp.zeros((40, LANES), F32)
         local_mix = coef[0:1, :] * parts[0]
         for j in range(1, 5):
             local_mix = local_mix + coef[j : j + 1, :] * parts[j]
-        red_send[0, 0:C, 0:C] = local_mix
+        red_send[0, 0:16, 0:C] = local_mix[0:16]
+        red_send[0, 0:16, C : 2 * C] = local_mix[16:32]
+        red_send[0, 0:16, 2 * C :] = jnp.zeros((16, 2 * C), F32)
         for j in range(5):
-            red_send[0, C + j : C + j + 1, 0:C] = jnp.sum(mix * parts[j], axis=0, keepdims=True)
+            red_send[0, j : j + 1, 2 * C : 3 * C] = jnp.sum(
+                mix * parts[j], axis=0, keepdims=True
+            )
 
     def place(phase):
         stride, size = phases[phase]
@@ -482,12 +495,11 @@
         ],
         axis=1,
     ).reshape(groups_y * 2 * YL, LANES)
+    tree_take(0)
+    tree_send(1)
     each_far(second)
     own_rows = pltpu.make_async_copy(rows(sbuf2, gy, 2 * YL), rows(lines_out, gy, 2 * YL), out_sem.at[0])
     own_rows.start()
-
-    tree_take(0)
-    tree_send(1)
 
     def outer_step(step, carry):
         shift = lax.rem(NK - step * 32, NK)
@@ -548,13 +560,20 @@
 def result_kernel(
     lines, sten, spectral, red, wx_ref,
     grad_input, grad_spectral, grad_mix, grad_coef,
-    cells, out_sem,
+    cells, field, mix_out, coef_out, out_sem,
 ):
     modes_x = wx_ref.shape[0] // 2
     out = pltpu.make_async_copy(spectral, grad_spectral, out_sem.at[0])
     out.start()
-    grad_mix[...] = red[0:C, 0:C]
-    grad_coef[...] = red[C : C + 5, 0:C]
+    mix_out[0:16, :] = red[:, 0:C]
+    mix_out[16:32, :] = red[:, C : 2 * C]
+    coef_out[...] = red[0:5, 2 * C : 3 * C]
+    small = [
+        pltpu.make_async_copy(mix_out, grad_mix, out_sem.at[1]),
+        pltpu.make_async_copy(coef_out, grad_coef, out_sem.at[2]),
+    ]
+    for copy in small:
+        copy.start()
     spread = jnp.concatenate(
         [
             jnp.concatenate(
@@ -570,10 +589,14 @@
             cells[half, pl.ds(y, LANES, stride=YL), :] = result[
                 y * LANES : (y + 1) * LANES, half * LANES : (half + 1) * LANES
             ]
+    planes = []
     for z in range(ZL):
         total = plane(cells, z * 256, 256) + plane(sten, z * 256, 256)
-        grad_input[:, z] = total.reshape(C, YL, NX)
-    out.wait()
+        field[z] = total.reshape(C, YL, NX)
+        planes.append(pltpu.make_async_copy(field.at[z], grad_input.at[:, z], out_sem.at[3 + z]))
+        planes[-1].start()
+    for copy in planes + small + [out]:
+        copy.wait()
 
 
 def per_device(input_field, pre_activation, cotangent, spectral_weights, mix_weights, coefficients):
@@ -604,11 +627,17 @@
             pltpu.VMEM((2 * rows_y, LANES), F32),
             pltpu.VMEM((2, ZL * 256, LANES), F32),
             pltpu.VMEM((2, NK, C, C), F32),
-            pltpu.VMEM((40, LANES), F32),
+            pltpu.VMEM((16, LANES), F32),
         ),
-        in_specs=[hbm] * 4 + [vmem] * 6,
+        in_specs=[hbm] * 10,
         out_specs=(vmem,) * 4,
         scratch_shapes=[
+            pltpu.VMEM((C, C), F32),
+            pltpu.VMEM((5, C), F32),
+            pltpu.VMEM(wx.shape, F32),
+            pltpu.VMEM(wy.shape, F32),
+            pltpu.VMEM(wy.T.shape, F32),
+            pltpu.VMEM(tw.shape, F32),
             pltpu.VMEM((C, ZL, YL, NX), F32),
             pltpu.VMEM((C, ZL, YL, NX), F32),
             pltpu.VMEM((C, ZL, YL, NX), F32),
@@ -631,9 +660,9 @@
             pltpu.VMEM((2, NK, LANES), F32),
             pltpu.VMEM((2, C, NK), F32),
             pltpu.VMEM((2, NK, LANES), F32),
-            pltpu.VMEM((len(phases), 40, LANES), F32),
-            pltpu.VMEM((len(phases), 8, 40, LANES), F32),
-            dma((4,)),
+            pltpu.VMEM((len(phases), 16, LANES), F32),
+            pltpu.VMEM((len(phases), 8, 16, LANES), F32),
+            dma((10,)),
             dma((groups_y,)), dma((groups_y,)), dma((groups_y,)), dma((groups_y,)),
             dma((groups_z,)), dma((groups_z,)), dma((groups_z,)), dma((groups_z,)),
             dma((4,)), dma((4,)),
@@ -662,10 +691,13 @@
             sds((5, C), F32),
         ),
         in_specs=[vmem] * 5,
-        out_specs=(vmem, hbm, vmem, vmem),
+        out_specs=(hbm,) * 4,
         scratch_shapes=[
             pltpu.VMEM((2, ZL * 256, LANES), F32),
-            dma((1,)),
+            pltpu.VMEM((ZL, C, YL, NX), F32),
+            pltpu.VMEM((C, C), F32),
+            pltpu.VMEM((5, C), F32),
+            dma((3 + ZL,)),
         ],
         compiler_params=pltpu.CompilerParams(vmem_limit_bytes=24 << 20),
     )(lines, sten, spectral, red, jnp.asarray(wx))

time: 47.9 us -> 43.6 us (0.910); the launches traced: 47 us -> 43.4 us
  Pallas kernels: 46.4 us -> 42.7 us
    pallas_call x1, Pallas kernels: 43.3 us -> 40.3 us  [per_device(): pl.pallas_call(functools.partial(exchange_kernel, groups_y, groups_z, pha...]
    pallas_call x1, Pallas kernels: 3.05 us -> 2.42 us  [per_device(): pl.pallas_call(result_kernel, name='result', out_shape=(sds((C, ZL, YL, N...]
where the time goes in v2:
time: 43.6 us; the launch traced here: 43.4 us
  Pallas kernels  42.7 us (98%)
  between operations  0.66 us (2%)
    pallas_call x1, Pallas kernels, per_device(): pl.pallas_call(functools.partial(exchange_kernel, groups_y, groups_z, pha...  40.3 us
    pallas_call x1, Pallas kernels, per_device(): pl.pallas_call(result_kernel, name='result', out_shape=(sds((C, ZL, YL, N...  2.42 us

profile of v2, /device:TPU:1, one launch (start us, length us, event | category | flops | bytes accessed | tf_op | source)
XLA Modules:
  0.0 43.4 jit_solution(5229844976440346990)
XLA Ops:
  0.6 0.0 copy-start
  0.6 40.3 %exchange.1 = (f32[512,128]{1,0:T(8,128)S(1)}, f32[2,1024,128]{2,1,0:T(8,128)S(1)}, f32[2,128,32,32]{3,2,1,0:T(8,128)S(1)}, f32[16,128]{1,0:T(8,128)S(1)}) custom-call(f32[32,4,8,256]{3,2,1,0:T(8,128)} %inp_hbm.1, f32[32,4,8,256]{3,2,1,0:T(8,128)} %pre_hbm.1, f32[32,4,8,256]{3,2,1,0:T(8,128)} %cot_hbm.1, f32[2,128,32,32]{3,2,1,0:T(8,128)} %bitcast.4, ...), custom_call_target="tpu_custom_call" | custom-call | tf_op jit(solution)/shard_map/exchange/pallas_call | solution.py:623
  41.0 0.0 copy-done
  41.0 2.4 %result.1 = (f32[32,4,8,256]{3,2,1,0:T(8,128)}, f32[2,128,32,32]{3,2,1,0:T(8,128)}, f32[32,32]{1,0:T(8,128)}, f32[5,32]{1,0:T(8,128)}) custom-call(f32[512,128]{1,0:T(8,128)S(1)} %get-tuple-element.12.lines, f32[2,1024,128]{2,1,0:T(8,128)S(1)} %get-tuple-element.13.sten, f32[2,128,32,32]{3,2,1,0:T(8,128)S(1)} %get-tuple-element.14.spectral, ...), custom_call_target="tpu_custom_call" | custom-call | tf_op jit(solution)/shard_map/result/pallas_call | solution.py:684
Async XLA Ops:
  0.6 40.3 %copy-start = (f32[64,256]{1,0:T(8,128)S(1)}, f32[64,256]{1,0:T(8,128)}, u32[]{:S(2)}) copy-start(f32[64,256]{1,0:T(8,128)} %constant.8.clone.wx_hbm.wx_ref) | copy-start | bytes 196612

commit v3 on v2

--- a/solution.py
+++ b/solution.py
@@ -103,7 +103,7 @@
     inp_hbm, pre_hbm, cot_hbm, wts_hbm, mix_hbm, coef_hbm, wx_hbm, wy_hbm, wyt_hbm, tw_hbm,
     lines_out, sten, spectral, red_sum,
     mix_ref, coef_ref, wx_ref, wy_ref, wyt_ref, tw_ref, inp4, pre4, cot4, wts, inp2, slo2, sbuf, rbuf, zsend, zrecv, zsend2, zrecv2, sbuf2,
-    hy_send, hy_recv, hz_recv, hid, gram, hin, hsl, hslt, dual, red_send, red_recv,
+    hy_send, hy_recv, hz_recv, hid, gram, packed, hin, hsl, hslt, dual, red_send, red_recv,
     load_sem, s1, r1, s2, r2, sz, rz, sz2, rz2, hs_sem, hr_sem, sr, rr, out_sem,
 ):
     gz = lax.axis_index("gz")
@@ -390,6 +390,17 @@
         else:
             red_sum[...] = total * (1.0 / 1024.0)
 
+    load(3, wts_hbm, wts).wait()
+
+    def pack_step(group, carry):
+        q, j = group // 8, lax.rem(group, 8)
+        for part in range(2):
+            for m in range(4):
+                packed[part, group, :, m * C : (m + 1) * C] = wts[part, (q + 4 * m) * 8 + j]
+        return carry
+
+    lax.fori_loop(0, 32, pack_step, 0)
+
     each(first_in, "wait_recv")
     received = rbuf[...].reshape(groups_y, 4, YL, LANES)
     received = jnp.concatenate(
@@ -436,19 +447,25 @@
     for part in range(2):
         hslt[part] = hsl[part].T[0:C, :]
 
-    load(3, wts_hbm, wts).wait()
-
-    def dual_step(step, carry):
-        shift = lax.rem(NK - step * 32, NK)
+    for copy, _, takes in halos:
+        pl.when(takes)(copy.wait_recv)
+    moments()
+    tree_send(0)
+
+    lane = iota((C, LANES), 1)
+
+    def dual_step(q, carry):
+        shift = lax.rem(NK - q * 8, NK)
         slope_re = pltpu.roll(hslt[0], shift, 1)
         slope_im = pltpu.roll(hslt[1], shift, 1)
-        for j in range(32):
-            k = step * 32 + j
-            s_re = jnp.broadcast_to(slope_re[:, j : j + 1], (C, C))
-            s_im = jnp.broadcast_to(slope_im[:, j : j + 1], (C, C))
-            w_re, w_im = wts[0, k], wts[1, k]
-            dual[0, pl.ds(k, 1), 0:C] = jnp.sum(w_re * s_re + w_im * s_im, axis=0, keepdims=True)
-            dual[1, pl.ds(k, 1), 0:C] = jnp.sum(w_re * s_im - w_im * s_re, axis=0, keepdims=True)
+        for j in range(8):
+            group = q * 8 + j
+            spread = lax.bitwise_and(lane, 96) + j
+            s_re = jnp.take_along_axis(slope_re, spread, axis=1)
+            s_im = jnp.take_along_axis(slope_im, spread, axis=1)
+            w_re, w_im = packed[0, group], packed[1, group]
+            dual[0, pl.ds(group, 1), :] = jnp.sum(w_re * s_re + w_im * s_im, axis=0, keepdims=True)
+            dual[1, pl.ds(group, 1), :] = jnp.sum(w_re * s_im - w_im * s_re, axis=0, keepdims=True)
         return carry
 
     lax.fori_loop(0, 4, dual_step, 0)
@@ -457,20 +474,26 @@
     v_re, v_im = [], []
     for k in range(4):
         u_re, u_im = dft4(
-            [dual[0, pl.ds((k + 4 * m) * 8, 8), :] for m in range(4)],
-            [dual[1, pl.ds((k + 4 * m) * 8, 8), :] for m in range(4)],
+            *(
+                [dual[part, k * 8 : k * 8 + 8, :]]
+                + [
+                    pltpu.roll(dual[part, k * 8 : k * 8 + 8, :], LANES - 32 * m, 1)
+                    for m in range(1, 4)
+                ]
+                for part in range(2)
+            ),
             1,
         )
-        packed = []
+        turned = []
         for u in (u_re, u_im):
             value = u[0]
             for s in range(1, 4):
                 value = jnp.where(block == s, pltpu.roll(u[s], 32 * s, 1), value)
-            packed.append(value)
+            turned.append(value)
         if k:
-            packed = turn(packed[0], packed[1], cos_z[k], sin_z[k], 1)
-        v_re.append(packed[0])
-        v_im.append(packed[1])
+            turned = turn(turned[0], turned[1], cos_z[k], sin_z[k], 1)
+        v_re.append(turned[0])
+        v_im.append(turned[1])
     v_re, v_im = dft4(v_re, v_im, 1)
     for q in range(4):
         zsend2[q * 8 : q * 8 + 8, 0:LANES] = v_re[q]
@@ -478,10 +501,8 @@
     for i in range(1, groups_z):
         across(zsend2, zrecv2, sz2, rz2, i, False).start()
     zrecv2[mine, :] = zsend2[mine, :]
-    for copy, _, takes in halos:
-        pl.when(takes)(copy.wait_recv)
-    moments()
-    tree_send(0)
+    tree_take(0)
+    tree_send(1)
     for i in range(1, groups_z):
         across(zsend2, zrecv2, sz2, rz2, i, True).wait_recv()
 
@@ -495,8 +516,6 @@
         ],
         axis=1,
     ).reshape(groups_y * 2 * YL, LANES)
-    tree_take(0)
-    tree_send(1)
     each_far(second)
     own_rows = pltpu.make_async_copy(rows(sbuf2, gy, 2 * YL), rows(lines_out, gy, 2 * YL), out_sem.at[0])
     own_rows.start()
@@ -656,10 +675,11 @@
             pltpu.VMEM((2, 2, 256, LANES), F32),
             pltpu.VMEM((6, 256, NX), F32),
             pltpu.VMEM((3, 256, 256), F32),
+            pltpu.VMEM((2, 32, C, LANES), F32),
             pltpu.VMEM((2, NK, LANES), F32),
             pltpu.VMEM((2, NK, LANES), F32),
             pltpu.VMEM((2, C, NK), F32),
-            pltpu.VMEM((2, NK, LANES), F32),
+            pltpu.VMEM((2, 32, LANES), F32),
             pltpu.VMEM((len(phases), 16, LANES), F32),
             pltpu.VMEM((len(phases), 8, 16, LANES), F32),
             dma((10,)),

time: 43.6 us -> 41.8 us (0.959)
  Pallas kernels: 42.7 us -> 41.1 us
    pallas_call x1, Pallas kernels: 40.3 us -> 38.6 us  [per_device(): pl.pallas_call(functools.partial(exchange_kernel, groups_y, groups_z, pha...]
where the time goes in v3:
time: 41.8 us; the launch traced here: 41.7 us
  Pallas kernels  41.1 us (98%)
  between operations  0.66 us (2%)
    pallas_call x1, Pallas kernels, per_device(): pl.pallas_call(functools.partial(exchange_kernel, groups_y, groups_z, pha...  38.6 us
    pallas_call x1, Pallas kernels, per_device(): pl.pallas_call(result_kernel, name='result', out_shape=(sds((C, ZL, YL, N...  2.42 us

profile of v3, /device:TPU:1, one launch (start us, length us, event | category | flops | bytes accessed | tf_op | source)
XLA Modules:
  0.0 41.7 jit_solution(8271430566467367973)
XLA Ops:
  0.6 0.0 copy-start
  0.6 38.6 %exchange.1 = (f32[512,128]{1,0:T(8,128)S(1)}, f32[2,1024,128]{2,1,0:T(8,128)S(1)}, f32[2,128,32,32]{3,2,1,0:T(8,128)S(1)}, f32[16,128]{1,0:T(8,128)S(1)}) custom-call(f32[32,4,8,256]{3,2,1,0:T(8,128)} %inp_hbm.1, f32[32,4,8,256]{3,2,1,0:T(8,128)} %pre_hbm.1, f32[32,4,8,256]{3,2,1,0:T(8,128)} %cot_hbm.1, f32[2,128,32,32]{3,2,1,0:T(8,128)} %bitcast.4, ...), custom_call_target="tpu_custom_call" | custom-call | tf_op jit(solution)/shard_map/exchange/pallas_call | solution.py:642
  39.3 0.0 copy-done
  39.3 2.4 %result.1 = (f32[32,4,8,256]{3,2,1,0:T(8,128)}, f32[2,128,32,32]{3,2,1,0:T(8,128)}, f32[32,32]{1,0:T(8,128)}, f32[5,32]{1,0:T(8,128)}) custom-call(f32[512,128]{1,0:T(8,128)S(1)} %get-tuple-element.12.lines, f32[2,1024,128]{2,1,0:T(8,128)S(1)} %get-tuple-element.13.sten, f32[2,128,32,32]{3,2,1,0:T(8,128)S(1)} %get-tuple-element.14.spectral, ...), custom_call_target="tpu_custom_call" | custom-call | tf_op jit(solution)/shard_map/result/pallas_call | solution.py:704
Async XLA Ops:
  0.6 38.7 %copy-start = (f32[64,256]{1,0:T(8,128)S(1)}, f32[64,256]{1,0:T(8,128)}, u32[]{:S(2)}) copy-start(f32[64,256]{1,0:T(8,128)} %constant.8.clone.wx_hbm.wx_ref) | copy-start | bytes 196612

commit v4 on v3

--- a/solution.py
+++ b/solution.py
@@ -103,7 +103,7 @@
     inp_hbm, pre_hbm, cot_hbm, wts_hbm, mix_hbm, coef_hbm, wx_hbm, wy_hbm, wyt_hbm, tw_hbm,
     lines_out, sten, spectral, red_sum,
     mix_ref, coef_ref, wx_ref, wy_ref, wyt_ref, tw_ref, inp4, pre4, cot4, wts, inp2, slo2, sbuf, rbuf, zsend, zrecv, zsend2, zrecv2, sbuf2,
-    hy_send, hy_recv, hz_recv, hid, gram, packed, hin, hsl, hslt, dual, red_send, red_recv,
+    hy_send, hy_recv, hz_recv, hid, inner, packed, hin, hsl, hslt, dual, red_send, red_recv,
     load_sem, s1, r1, s2, r2, sz, rz, sz2, rz2, hs_sem, hr_sem, sr, rr, out_sem,
 ):
     gz = lax.axis_index("gz")
@@ -309,41 +309,58 @@
         put_plane(sten, z * 256, both[0:256])
         hid[z + 1] = both[256:512]
     own = [split(plane(slo2, z * 256, 256)) for z in range(ZL)]
-    for kind, shift in enumerate((0, -1, 1)):
+    grams = []
+    for shift in (0, -1, 1):
         total = None
         for z in range(ZL):
             if 0 <= z + shift < ZL:
                 term = gram_of(own[z + shift], z)
                 total = term if total is None else total + term
-        gram[kind] = total
-
-    def moments():
-        gram_0 = gram[0]
-        gram_up = gram[1] + gram_of(outside(0), 0)
-        gram_down = gram[2] + gram_of(outside(1), ZL - 1)
-        before_y, after_y = outside(2), outside(3)
-        edge = None
-        for z in range(ZL):
-            at = slice(z * C, (z + 1) * C)
-            term = gram_of(jnp.concatenate([before_y[at], after_y[at]], axis=0), z)
-            edge = term if z == 0 else edge + term
-        pieces = jnp.concatenate(
+        grams.append(total)
+    pieces = jnp.concatenate(
+        [
+            jnp.where(same, grams[0], 0.0),
+            jnp.where(col_y == row_y + 1, grams[0], 0.0),
+            jnp.where(col_y == row_y - 1, grams[0], 0.0),
+            jnp.where(same, grams[1], 0.0),
+            jnp.where(same, grams[2], 0.0),
+        ],
+        axis=1,
+    )
+    summed = dot3(gather, pieces, NN)
+    sums = [summed[:, j * 256 : (j + 1) * 256] for j in range(5)]
+    inner[...] = dot3(jnp.concatenate(sums, axis=0), expand, NN)
+
+    def along(ref, starts, stride):
+        return jnp.concatenate(
             [
-                jnp.where(same, gram_0, 0.0),
-                jnp.where(col_y == row_y + 1, gram_0, 0.0),
-                jnp.where(col_y == row_y - 1, gram_0, 0.0),
-                jnp.where(same, gram_up, 0.0),
-                jnp.where(same, gram_down, 0.0),
+                ref[half, pl.ds(start, C, stride=stride), :]
+                for start in starts
+                for half in range(2)
             ],
             axis=1,
         )
-        summed = dot3(gather, pieces, NN)
-        edge_y = col_y[0:C]
-        sums = [summed[:, j * 256 : (j + 1) * 256] for j in range(5)]
-        sums[1] = sums[1] + jnp.where(edge_y == 0, edge[0:C], 0.0)
-        sums[2] = sums[2] + jnp.where(edge_y == YL - 1, edge[C : 2 * C], 0.0)
-        every = dot3(jnp.concatenate(sums, axis=0), expand, NN)
-        parts = [every[j * C : (j + 1) * C] for j in range(5)]
+
+    def moments():
+        planes_y = [z * 256 for z in range(ZL)]
+        rows_z = [z * C for z in range(ZL)]
+        lines_y = list(range(YL))
+        last = (ZL - 1) * 256
+        outer = {
+            1: (along(hy_recv.at[0], rows_z, 1), along(inp2, planes_y, YL)),
+            2: (
+                along(hy_recv.at[1], rows_z, 1),
+                along(inp2, [start + YL - 1 for start in planes_y], YL),
+            ),
+            3: (along(hz_recv.at[0], lines_y, YL), along(inp2, lines_y, YL)),
+            4: (
+                along(hz_recv.at[1], lines_y, YL),
+                along(inp2, [last + y for y in lines_y], YL),
+            ),
+        }
+        parts = [inner[j * C : (j + 1) * C, :] for j in range(5)]
+        for j, (left, right) in outer.items():
+            parts[j] = parts[j] + dot3(left, right, NT)
         local_mix = coef[0:1, :] * parts[0]
         for j in range(1, 5):
             local_mix = local_mix + coef[j : j + 1, :] * parts[j]
@@ -674,7 +691,7 @@
             pltpu.VMEM((2, 2, ZL * C, LANES), F32),
             pltpu.VMEM((2, 2, 256, LANES), F32),
             pltpu.VMEM((6, 256, NX), F32),
-            pltpu.VMEM((3, 256, 256), F32),
+            pltpu.VMEM((5 * C, C), F32),
             pltpu.VMEM((2, 32, C, LANES), F32),
             pltpu.VMEM((2, NK, LANES), F32),
             pltpu.VMEM((2, NK, LANES), F32),

time: 41.8 us -> 40.8 us (0.976)
  Pallas kernels: 41.1 us -> 40 us
    pallas_call x1, Pallas kernels: 38.6 us -> 37.6 us  [per_device(): pl.pallas_call(functools.partial(exchange_kernel, groups_y, groups_z, pha...]
where the time goes in v4:
time: 40.8 us; the launch traced here: 40.7 us
  Pallas kernels  40 us (98%)
  between operations  0.66 us (2%)
    pallas_call x1, Pallas kernels, per_device(): pl.pallas_call(functools.partial(exchange_kernel, groups_y, groups_z, pha...  37.6 us
    pallas_call x1, Pallas kernels, per_device(): pl.pallas_call(result_kernel, name='result', out_shape=(sds((C, ZL, YL, N...  2.42 us

profile of v4, /device:TPU:1, one launch (start us, length us, event | category | flops | bytes accessed | tf_op | source)
XLA Modules:
  0.0 40.7 jit_solution(18371484617229785115)
XLA Ops:
  0.6 0.0 copy-start
  0.6 37.6 %exchange.1 = (f32[512,128]{1,0:T(8,128)S(1)}, f32[2,1024,128]{2,1,0:T(8,128)S(1)}, f32[2,128,32,32]{3,2,1,0:T(8,128)S(1)}, f32[16,128]{1,0:T(8,128)S(1)}) custom-call(f32[32,4,8,256]{3,2,1,0:T(8,128)} %inp_hbm.1, f32[32,4,8,256]{3,2,1,0:T(8,128)} %pre_hbm.1, f32[32,4,8,256]{3,2,1,0:T(8,128)} %cot_hbm.1, f32[2,128,32,32]{3,2,1,0:T(8,128)} %bitcast.4, ...), custom_call_target="tpu_custom_call" | custom-call | tf_op jit(solution)/shard_map/exchange/pallas_call | solution.py:659
  38.3 0.0 copy-done
  38.3 2.4 %result.1 = (f32[32,4,8,256]{3,2,1,0:T(8,128)}, f32[2,128,32,32]{3,2,1,0:T(8,128)}, f32[32,32]{1,0:T(8,128)}, f32[5,32]{1,0:T(8,128)}) custom-call(f32[512,128]{1,0:T(8,128)S(1)} %get-tuple-element.12.lines, f32[2,1024,128]{2,1,0:T(8,128)S(1)} %get-tuple-element.13.sten, f32[2,128,32,32]{3,2,1,0:T(8,128)S(1)} %get-tuple-element.14.spectral, ...), custom_call_target="tpu_custom_call" | custom-call | tf_op jit(solution)/shard_map/result/pallas_call | solution.py:721
Async XLA Ops:
  0.6 37.7 %copy-start = (f32[64,256]{1,0:T(8,128)S(1)}, f32[64,256]{1,0:T(8,128)}, u32[]{:S(2)}) copy-start(f32[64,256]{1,0:T(8,128)} %constant.8.clone.wx_hbm.wx_ref) | copy-start | bytes 196612

commit v5 on v4

--- a/solution.py
+++ b/solution.py
@@ -434,6 +434,10 @@
         across(zsend, zrecv, sz, rz, i, False).start()
     mine = pl.ds(pl.multiple_of(gz * 8, 8), 8)
     zrecv[mine, :] = zsend[mine, :]
+    for copy, _, takes in halos:
+        pl.when(takes)(copy.wait_recv)
+    moments()
+    tree_send(0)
     for i in range(1, groups_z):
         across(zsend, zrecv, sz, rz, i, True).wait_recv()
 
@@ -464,11 +468,6 @@
     for part in range(2):
         hslt[part] = hsl[part].T[0:C, :]
 
-    for copy, _, takes in halos:
-        pl.when(takes)(copy.wait_recv)
-    moments()
-    tree_send(0)
-
     lane = iota((C, LANES), 1)
 
     def dual_step(q, carry):
@@ -534,6 +533,9 @@
         axis=1,
     ).reshape(groups_y * 2 * YL, LANES)
     each_far(second)
+    tree_take(1)
+    if len(phases) > 2:
+        tree_send(2)
     own_rows = pltpu.make_async_copy(rows(sbuf2, gy, 2 * YL), rows(lines_out, gy, 2 * YL), out_sem.at[0])
     own_rows.start()
 
@@ -552,9 +554,6 @@
         return carry
 
     lax.fori_loop(0, 4, outer_step, 0)
-    tree_take(1)
-    if len(phases) > 2:
-        tree_send(2)
     hid[0] = dot3(plain, outside(0), NN)
     hid[5] = dot3(plain, outside(1), NN)
     for z in range(ZL):

time: 40.8 us -> 40.2 us (0.985)
  Pallas kernels: 40 us -> 39.4 us
    pallas_call x1, Pallas kernels: 37.6 us -> 37 us  [per_device(): pl.pallas_call(functools.partial(exchange_kernel, groups_y, groups_z, pha...]
where the time goes in v5:
time: 40.2 us; the launch traced here: 40.1 us
  Pallas kernels  39.4 us (98%)
  between operations  0.66 us (2%)
    pallas_call x1, Pallas kernels, per_device(): pl.pallas_call(functools.partial(exchange_kernel, groups_y, groups_z, pha...  37 us
    pallas_call x1, Pallas kernels, per_device(): pl.pallas_call(result_kernel, name='result', out_shape=(sds((C, ZL, YL, N...  2.42 us

profile of v5, /device:TPU:1, one launch (start us, length us, event | category | flops | bytes accessed | tf_op | source)
XLA Modules:
  0.0 40.1 jit_solution(14269908067765643073)
XLA Ops:
  0.6 0.0 copy-start
  0.6 37.0 %exchange.1 = (f32[512,128]{1,0:T(8,128)S(1)}, f32[2,1024,128]{2,1,0:T(8,128)S(1)}, f32[2,128,32,32]{3,2,1,0:T(8,128)S(1)}, f32[16,128]{1,0:T(8,128)S(1)}) custom-call(f32[32,4,8,256]{3,2,1,0:T(8,128)} %inp_hbm.1, f32[32,4,8,256]{3,2,1,0:T(8,128)} %pre_hbm.1, f32[32,4,8,256]{3,2,1,0:T(8,128)} %cot_hbm.1, f32[2,128,32,32]{3,2,1,0:T(8,128)} %bitcast.4, ...), custom_call_target="tpu_custom_call" | custom-call | tf_op jit(solution)/shard_map/exchange/pallas_call | solution.py:658
  37.7 0.0 copy-done
  37.7 2.4 %result.1 = (f32[32,4,8,256]{3,2,1,0:T(8,128)}, f32[2,128,32,32]{3,2,1,0:T(8,128)}, f32[32,32]{1,0:T(8,128)}, f32[5,32]{1,0:T(8,128)}) custom-call(f32[512,128]{1,0:T(8,128)S(1)} %get-tuple-element.12.lines, f32[2,1024,128]{2,1,0:T(8,128)S(1)} %get-tuple-element.13.sten, f32[2,128,32,32]{3,2,1,0:T(8,128)S(1)} %get-tuple-element.14.spectral, ...), custom_call_target="tpu_custom_call" | custom-call | tf_op jit(solution)/shard_map/result/pallas_call | solution.py:720
Async XLA Ops:
  0.6 37.1 %copy-start = (f32[64,256]{1,0:T(8,128)S(1)}, f32[64,256]{1,0:T(8,128)}, u32[]{:S(2)}) copy-start(f32[64,256]{1,0:T(8,128)} %constant.8.clone.wx_hbm.wx_ref) | copy-start | bytes 196612

commit v6 on v5

--- a/solution.py
+++ b/solution.py
@@ -578,8 +578,6 @@
     if len(phases) > 2:
         tree_take(2)
 
-    each(second_in, "wait_recv")
-    own_rows.wait()
     each(first, "wait_send")
     each(second, "wait_send")
     for copy, sends, _ in halos:
@@ -590,6 +588,8 @@
     for phase in range(len(phases)):
         for i in range(1, place(phase)[0]):
             piece(phase, i, False).wait_send()
+    each(second_in, "wait_recv")
+    own_rows.wait()
 
 
 def result_kernel(

time: 40.2 us -> 40.2 us (level)
  no operation moved by 1% of the time
where the time goes in v6:
time: 40.2 us; the launch traced here: 40.1 us
  Pallas kernels  39.4 us (98%)
  between operations  0.66 us (2%)
    pallas_call x1, Pallas kernels, per_device(): pl.pallas_call(functools.partial(exchange_kernel, groups_y, groups_z, pha...  37 us
    pallas_call x1, Pallas kernels, per_device(): pl.pallas_call(result_kernel, name='result', out_shape=(sds((C, ZL, YL, N...  2.42 us

profile of v6, /device:TPU:1, one launch (start us, length us, event | category | flops | bytes accessed | tf_op | source)
XLA Modules:
  0.0 40.1 jit_solution(9984326432052931964)
XLA Ops:
  0.6 0.0 copy-start
  0.6 37.0 %exchange.1 = (f32[512,128]{1,0:T(8,128)S(1)}, f32[2,1024,128]{2,1,0:T(8,128)S(1)}, f32[2,128,32,32]{3,2,1,0:T(8,128)S(1)}, f32[16,128]{1,0:T(8,128)S(1)}) custom-call(f32[32,4,8,256]{3,2,1,0:T(8,128)} %inp_hbm.1, f32[32,4,8,256]{3,2,1,0:T(8,128)} %pre_hbm.1, f32[32,4,8,256]{3,2,1,0:T(8,128)} %cot_hbm.1, f32[2,128,32,32]{3,2,1,0:T(8,128)} %bitcast.4, ...), custom_call_target="tpu_custom_call" | custom-call | tf_op jit(solution)/shard_map/exchange/pallas_call | solution.py:658
  37.7 0.0 copy-done
  37.7 2.4 %result.1 = (f32[32,4,8,256]{3,2,1,0:T(8,128)}, f32[2,128,32,32]{3,2,1,0:T(8,128)}, f32[32,32]{1,0:T(8,128)}, f32[5,32]{1,0:T(8,128)}) custom-call(f32[512,128]{1,0:T(8,128)S(1)} %get-tuple-element.12.lines, f32[2,1024,128]{2,1,0:T(8,128)S(1)} %get-tuple-element.13.sten, f32[2,128,32,32]{3,2,1,0:T(8,128)S(1)} %get-tuple-element.14.spectral, ...), custom_call_target="tpu_custom_call" | custom-call | tf_op jit(solution)/shard_map/result/pallas_call | solution.py:720
Async XLA Ops:
  0.6 37.0 %copy-start = (f32[64,256]{1,0:T(8,128)S(1)}, f32[64,256]{1,0:T(8,128)}, u32[]{:S(2)}) copy-start(f32[64,256]{1,0:T(8,128)} %constant.8.clone.wx_hbm.wx_ref) | copy-start | bytes 196612
